TPU v7x, 32 devices: a whole 2x2x4 slice. The times are simulated.
32 devices in a mesh: sub: 4 (over z), wide: 8 (over y, x, core).
Axes of the slice: x: 2, y: 2, z: 4, core: 2. Of those that a mesh axis runs over, the one named last changes fastest.
Arguments:
- load_table: bfloat16 [4, 8, 16, 4, 128], P('sub', 'wide'), may hold values from -6 to 6
- load_column: int32 [64], replicated, may hold values from 0 to 15
- face_order: int32 [4, 8, 4], P('sub', 'wide'), may hold values from 0 to 3, each once within a row
- schur: bfloat16 [4, 8, 512, 512], P('sub', 'wide'), as said below
- neumann: bfloat16 [4, 8, 512, 512], P('sub', 'wide'), as said below
- coarse_basis: bfloat16 [4, 8, 4, 4, 128], P('sub', 'wide'), may hold values from -0.625 to 0.625
- corner_map: int32 [4, 8, 4], P('sub', 'wide'), may hold values from 0 to 47, as said below
- coarse_inverse: float32 [48, 48], P('wide'), as said below
Outputs:
- solution: float32 [4, 8, 4, 64, 128], P('sub', 'wide')
Inputs may be any that keep to these rules, and one draw needn't show every extreme that they name: `corner_map`: each subdomain's 4 entries are distinct; subdomains that meet at a corner of the grid of subdomains give it the same number, and different corners get different numbers, so (5) * (9) of the 48 numbers occur and the others belong to no corner. `coarse_inverse`: Symmetric. `schur`: Symmetric. `neumann`: Symmetric.
All inputs are finite; a program needn't handle non-finite values.
Results may differ from a plain program's by a relative error of at most 0.0014.
Values sent between devices are 32-bit elements; how exact they have to be, the bound alone decides.
A program may use at most 64 MiB of HBM per device.

v0:
```python
import jax
import jax.numpy as jnp
from jax import lax
from jax.sharding import PartitionSpec as P

ITERS = 3
damping = 0.3


def with_halo(cells, sides, width):
    for axis, dim in sides:
        count = lax.axis_size(axis)
        ends = count - 1
        head = lax.slice_in_dim(cells, 0, width, axis=dim)
        tail = lax.slice_in_dim(cells, cells.shape[dim] - width, cells.shape[dim], axis=dim)
        cells = jnp.concatenate(
            [
                lax.ppermute(tail, axis, [(i, (i + 1) % count) for i in range(ends)]),
                cells,
                lax.ppermute(head, axis, [((i + 1) % count, i) for i in range(ends)]),
            ],
            axis=dim,
        )
    return cells


def apply_local(vectors, operators, selector_half, selector_full):
    amount = vectors.shape[0]
    rhs_count = vectors.shape[3]
    face_width = vectors.shape[4]
    rounded = vectors.astype(jnp.bfloat16)
    blocked = jnp.einsum(
        "kcbf,kcfjn->kcjbn", selector_half, rounded, preferred_element_type=jnp.float32
    )
    blocked = blocked.astype(jnp.bfloat16).reshape(amount, 1, rhs_count, 4 * face_width)
    product = jnp.einsum("kcjm,kcmn->kcjn", blocked, operators, preferred_element_type=jnp.float32)
    product = product.reshape(amount, 1, rhs_count, 4, face_width)
    return jnp.einsum("kcbf,kcjbn->kcfjn", selector_full, product, precision=lax.Precision.HIGHEST)


def assemble(copies):
    side_stack = jnp.stack([copies[:, 0, 2], copies[:, 0, 3]], axis=0)
    side_halo = with_halo(side_stack, (("wide", 0),), 1)
    end_stack = jnp.stack([copies[0, 0, 0], copies[-1, 0, 1]], axis=0)
    end_halo = with_halo(end_stack, (("sub", 0),), 1)
    upper_faces = jnp.concatenate([end_halo[0:1], copies[:-1, 0, 1]], axis=0)
    lower_faces = jnp.concatenate([copies[1:, 0, 0], end_halo[3:4]], axis=0)
    north_sum = copies[:, 0, 0] + upper_faces
    south_sum = copies[:, 0, 1] + lower_faces
    west_sum = copies[:, 0, 2] + side_halo[0]
    east_sum = copies[:, 0, 3] + side_halo[3]
    return jnp.stack([north_sum, south_sum, west_sum, east_sum], axis=1)[:, None]


def coarse_solve(partial_value, coarse_inverse):
    assembled = lax.psum(partial_value, ("sub", "wide"))
    owned_rows = jnp.dot(assembled, coarse_inverse.T, precision=lax.Precision.HIGHEST)
    return lax.all_gather(owned_rows, "wide", axis=1, tiled=True)


def body(
    load_table, load_column, face_order, schur, neumann, coarse_basis, corner_map, coarse_inverse
):
    amount = schur.shape[0]
    pattern_count = load_table.shape[2]
    coarse_order = coarse_inverse.shape[1]
    selector_full = (face_order[..., :, None] == jnp.arange(4, dtype=jnp.int32)).astype(jnp.float32)
    selector_half = selector_full.astype(jnp.bfloat16)
    load_select = (load_column[:, None] == jnp.arange(pattern_count, dtype=jnp.int32)).astype(
        jnp.bfloat16
    )
    load_faces = jnp.einsum(
        "jl,kclfn->kcfjn", load_select, load_table, preferred_element_type=jnp.float32
    )
    row_ids = lax.axis_index("sub") * amount + jnp.arange(amount, dtype=jnp.int32)
    rows_total = amount * lax.axis_size("sub")
    column_index = lax.axis_index("wide") * jnp.ones((amount,), jnp.int32)
    cols_total = lax.axis_size("wide")
    half = jnp.float32(0.5)
    whole = jnp.float32(1.0)
    weights = jnp.stack(
        [
            jnp.where(row_ids > 0, half, whole),
            jnp.where(row_ids < rows_total - 1, half, whole),
            jnp.where(column_index > 0, half, whole),
            jnp.where(column_index < cols_total - 1, half, whole),
        ],
        axis=1,
    )[:, None, :, None, None]
    basis = coarse_basis.astype(jnp.float32)
    corner_marks = (corner_map[..., None] == jnp.arange(coarse_order, dtype=jnp.int32)).astype(
        jnp.float32
    )
    solution = jnp.zeros(load_faces.shape, jnp.float32)
    for iteration in range(ITERS):
        if iteration == 0:
            residual = assemble(load_faces)
        else:
            residual = assemble(
                load_faces - apply_local(solution, schur, selector_half, selector_full)
            )
        weighted = weights * residual
        restricted = jnp.einsum(
            "kcpfn,kcfjn->kcpj", basis, weighted, precision=lax.Precision.HIGHEST
        )
        partial_value = jnp.einsum(
            "kcpj,kcpg->jg", restricted, corner_marks, precision=lax.Precision.HIGHEST
        )
        neumann_part = apply_local(weighted, neumann, selector_half, selector_full)
        solved = coarse_solve(partial_value, coarse_inverse)
        picked = jnp.einsum("jg,kcpg->kcpj", solved, corner_marks, precision=lax.Precision.HIGHEST)
        correction = jnp.einsum("kcpj,kcpfn->kcfjn", picked, basis, precision=lax.Precision.HIGHEST)
        update = assemble(weights * (neumann_part + correction))
        solution = solution + damping * update
    return solution


def solution(mesh):
    in_specs = (
        P("sub", "wide", None, None, None),
        P(),
        P("sub", "wide", None),
        P("sub", "wide", None, None),
        P("sub", "wide", None, None),
        P("sub", "wide", None, None, None),
        P("sub", "wide", None),
        P("wide", None),
    )
    out_specs = P("sub", "wide", None, None, None)
    return jax.shard_map(body, mesh=mesh, in_specs=in_specs, out_specs=out_specs, check_vma=False)
```

profile of v0, /device:TPU:4, one launch (start us, length us, event | category | flops | bytes accessed | tf_op | source)
XLA Modules:
  0.0 250.2 jit_solution(4208679977386832550)
XLA Ops:
  0.9 3.5 %collective-permute-start = (f32[1,64,128]{2,1,0:T(8,128)S(1)}, f32[1,64,128]{2,1,0:T(8,128)S(1)}, u32[]{:S(2)}, u32[]{:S(2)}) collective-permute-start(f32[1,64,128]{2,1,0:T(8,128)S(1)} %get-tuple-element.47), channel_id=1, source_target_pairs={{0,8},{8,16},{16,24},{1,9},{9,17},{17,25},{2,10},{10,18},{18,26},{... | collective-permute-start | bytes 98312 | tf_op jit(solution)/shard_map/ppermute | solution.py:18
  4.4 1.9 collective-permute-start.2
  6.4 4.5 %collective-permute-start.3 = (f32[1,1,64,128]{3,2,1,0:T(8,128)S(1)}, f32[1,1,64,128]{3,2,1,0:T(8,128)S(1)}, u32[]{:S(2)}, u32[]{:S(2)}) collective-permute-start(f32[1,1,64,128]{3,2,1,0:T(8,128)S(1)} %get-tuple-element.49), channel_id=1, source_target_pairs={{1,0},{2,1},{3,2},{4,3},{5,4},{6,5},{7,6},{9,8},{10,9},{11,10},{12... | collective-permute-start | bytes 98312 | tf_op jit(solution)/shard_map/ppermute | solution.py:20
  13.6 3.1 %collective-permute-done.1 = f32[1,64,128]{2,1,0:T(8,128)S(1)} collective-permute-done((f32[1,64,128]{2,1,0:T(8,128)S(1)}, f32[1,64,128]{2,1,0:T(8,128)S(1)}, u32[]{:S(2)}, u32[]{:S(2)}) %collective-permute-start.1) | collective-permute-done | bytes 32800 | tf_op jit(solution)/shard_map/ppermute | solution.py:20
  19.6 40.5 %psum.21 = f32[64,48]{0,1:T(8,128)S(1)} all-reduce(f32[64,48]{0,1:T(8,128)S(1)} %fusion.44), channel_id=1, replica_groups=mesh['sub'=4,'wide'=8] {'sub','wide'}, use_global_device_ids=true, to_apply=%region_0.1 | all-reduce | flops 3072 | bytes 24576 | tf_op jit(solution)/shard_map/psum | solution.py:56
  60.2 9.0 %all-gather = f32[8,6,64]{2,1,0:T(8,128)S(1)} all-gather(f32[1,6,64]{2,1,0:T(8,128)S(1)} %convolution_bitcast_fusion.6), channel_id=1, replica_groups=mesh['sub'=4,'wide'=8] {'wide'}, dimensions={0}, use_global_device_ids=true | all-gather | bytes 13824 | tf_op jit(solution)/shard_map/all_gather | solution.py:58
  70.4 2.3 collective-permute-start.6
  72.6 4.2 %collective-permute-start.7 = (f32[1,1,64,128]{3,2,1,0:T(8,128)S(1)}, f32[1,1,64,128]{3,2,1,0:T(8,128)S(1)}, u32[]{:S(2)}, u32[]{:S(2)}) collective-permute-start(f32[1,1,64,128]{3,2,1,0:T(8,128)S(1)} %get-tuple-element.41), channel_id=1, source_target_pairs={{1,0},{2,1},{3,2},{4,3},{5,4},{6,5},{7,6},{9,8},{10,9},{11,10},{12... | collective-permute-start | bytes 98312 | tf_op jit(solution)/shard_map/ppermute | solution.py:20
  77.1 2.2 collective-permute-start.4
  79.2 1.3 collective-permute-start.5
  80.8 4.2 %collective-permute-done.5 = f32[1,64,128]{2,1,0:T(8,128)S(1)} collective-permute-done((f32[1,64,128]{2,1,0:T(8,128)S(1)}, f32[1,64,128]{2,1,0:T(8,128)S(1)}, u32[]{:S(2)}, u32[]{:S(2)}) %collective-permute-start.5) | collective-permute-done | bytes 32800 | tf_op jit(solution)/shard_map/ppermute | solution.py:20
  86.0 1.9 collective-permute-start.10
  87.9 4.5 %collective-permute-start.11 = (f32[1,1,64,128]{3,2,1,0:T(8,128)S(1)}, f32[1,1,64,128]{3,2,1,0:T(8,128)S(1)}, u32[]{:S(2)}, u32[]{:S(2)}) collective-permute-start(f32[1,1,64,128]{3,2,1,0:T(8,128)S(1)} %get-tuple-element.33), channel_id=1, source_target_pairs={{1,0},{2,1},{3,2},{4,3},{5,4},{6,5},{7,6},{9,8},{10,9},{11,10},{12... | collective-permute-start | bytes 98312 | tf_op jit(solution)/shard_map/ppermute | solution.py:20
  92.5 3.1 %collective-permute-start.8 = (f32[1,64,128]{2,1,0:T(8,128)S(1)}, f32[1,64,128]{2,1,0:T(8,128)S(1)}, u32[]{:S(2)}, u32[]{:S(2)}) collective-permute-start(f32[1,64,128]{2,1,0:T(8,128)S(1)} %get-tuple-element.31), channel_id=1, source_target_pairs={{0,8},{8,16},{16,24},{1,9},{9,17},{17,25},{2,10},{10,18},{18,26},{... | collective-permute-start | bytes 98312 | tf_op jit(solution)/shard_map/ppermute | solution.py:18
  97.1 4.2 %collective-permute-done.9 = f32[1,64,128]{2,1,0:T(8,128)S(1)} collective-permute-done((f32[1,64,128]{2,1,0:T(8,128)S(1)}, f32[1,64,128]{2,1,0:T(8,128)S(1)}, u32[]{:S(2)}, u32[]{:S(2)}) %collective-permute-start.9) | collective-permute-done | bytes 32800 | tf_op jit(solution)/shard_map/ppermute | solution.py:20
  102.3 40.3 %psum.22 = f32[64,48]{0,1:T(8,128)S(1)} all-reduce(f32[64,48]{0,1:T(8,128)S(1)} %fusion.43), channel_id=1, replica_groups=mesh['sub'=4,'wide'=8] {'sub','wide'}, use_global_device_ids=true, to_apply=%region_1.2 | all-reduce | flops 3072 | bytes 24576 | tf_op jit(solution)/shard_map/psum | solution.py:56
  142.7 9.5 %all-gather.1 = f32[8,6,64]{2,1,0:T(8,128)S(1)} all-gather(f32[1,6,64]{2,1,0:T(8,128)S(1)} %convolution_bitcast_fusion.5), channel_id=1, replica_groups=mesh['sub'=4,'wide'=8] {'wide'}, dimensions={0}, use_global_device_ids=true | all-gather | bytes 13824 | tf_op jit(solution)/shard_map/all_gather | solution.py:58
  153.3 2.3 collective-permute-start.14
  155.5 4.2 %collective-permute-start.15 = (f32[1,1,64,128]{3,2,1,0:T(8,128)S(1)}, f32[1,1,64,128]{3,2,1,0:T(8,128)S(1)}, u32[]{:S(2)}, u32[]{:S(2)}) collective-permute-start(f32[1,1,64,128]{3,2,1,0:T(8,128)S(1)} %get-tuple-element.25), channel_id=1, source_target_pairs={{1,0},{2,1},{3,2},{4,3},{5,4},{6,5},{7,6},{9,8},{10,9},{11,10},{12... | collective-permute-start | bytes 98312 | tf_op jit(solution)/shard_map/ppermute | solution.py:20
  159.8 1.9 collective-permute-start.12
  163.3 4.2 %collective-permute-done.13 = f32[1,64,128]{2,1,0:T(8,128)S(1)} collective-permute-done((f32[1,64,128]{2,1,0:T(8,128)S(1)}, f32[1,64,128]{2,1,0:T(8,128)S(1)}, u32[]{:S(2)}, u32[]{:S(2)}) %collective-permute-start.13) | collective-permute-done | bytes 32800 | tf_op jit(solution)/shard_map/ppermute | solution.py:20
  168.5 1.9 collective-permute-start.18
  170.4 4.5 %collective-permute-start.19 = (f32[1,1,64,128]{3,2,1,0:T(8,128)S(1)}, f32[1,1,64,128]{3,2,1,0:T(8,128)S(1)}, u32[]{:S(2)}, u32[]{:S(2)}) collective-permute-start(f32[1,1,64,128]{3,2,1,0:T(8,128)S(1)} %get-tuple-element.17), channel_id=1, source_target_pairs={{1,0},{2,1},{3,2},{4,3},{5,4},{6,5},{7,6},{9,8},{10,9},{11,10},{12... | collective-permute-start | bytes 98312 | tf_op jit(solution)/shard_map/ppermute | solution.py:20
  175.0 2.6 %collective-permute-start.16 = (f32[1,64,128]{2,1,0:T(8,128)S(1)}, f32[1,64,128]{2,1,0:T(8,128)S(1)}, u32[]{:S(2)}, u32[]{:S(2)}) collective-permute-start(f32[1,64,128]{2,1,0:T(8,128)S(1)} %get-tuple-element.15), channel_id=1, source_target_pairs={{0,8},{8,16},{16,24},{1,9},{9,17},{17,25},{2,10},{10,18},{18,26},{... | collective-permute-start | bytes 98312 | tf_op jit(solution)/shard_map/ppermute | solution.py:18
  179.1 4.2 %collective-permute-done.17 = f32[1,64,128]{2,1,0:T(8,128)S(1)} collective-permute-done((f32[1,64,128]{2,1,0:T(8,128)S(1)}, f32[1,64,128]{2,1,0:T(8,128)S(1)}, u32[]{:S(2)}, u32[]{:S(2)}) %collective-permute-start.17) | collective-permute-done | bytes 32800 | tf_op jit(solution)/shard_map/ppermute | solution.py:20
  184.9 40.3 %psum.23 = f32[64,48]{0,1:T(8,128)S(1)} all-reduce(f32[64,48]{0,1:T(8,128)S(1)} %fusion.42), channel_id=1, replica_groups=mesh['sub'=4,'wide'=8] {'sub','wide'}, use_global_device_ids=true, to_apply=%region_2.3 | all-reduce | flops 3072 | bytes 24576 | tf_op jit(solution)/shard_map/psum | solution.py:56
  225.2 9.5 %all-gather.2 = f32[8,6,64]{2,1,0:T(8,128)S(1)} all-gather(f32[1,6,64]{2,1,0:T(8,128)S(1)} %convolution_bitcast_fusion.4), channel_id=1, replica_groups=mesh['sub'=4,'wide'=8] {'wide'}, dimensions={0}, use_global_device_ids=true | all-gather | bytes 13824 | tf_op jit(solution)/shard_map/all_gather | solution.py:58
  235.3 2.3 collective-permute-start.22
  237.5 4.2 %collective-permute-start.23 = (f32[1,1,64,128]{3,2,1,0:T(8,128)S(1)}, f32[1,1,64,128]{3,2,1,0:T(8,128)S(1)}, u32[]{:S(2)}, u32[]{:S(2)}) collective-permute-start(f32[1,1,64,128]{3,2,1,0:T(8,128)S(1)} %get-tuple-element.9), channel_id=1, source_target_pairs={{1,0},{2,1},{3,2},{4,3},{5,4},{6,5},{7,6},{9,8},{10,9},{11,10},{12... | collective-permute-start | bytes 98312 | tf_op jit(solution)/shard_map/ppermute | solution.py:20
  241.7 1.9 collective-permute-start.20
  243.7 1.3 collective-permute-start.21
  245.2 4.2 %collective-permute-done.21 = f32[1,64,128]{2,1,0:T(8,128)S(1)} collective-permute-done((f32[1,64,128]{2,1,0:T(8,128)S(1)}, f32[1,64,128]{2,1,0:T(8,128)S(1)}, u32[]{:S(2)}, u32[]{:S(2)}) %collective-permute-start.21) | collective-permute-done | bytes 32800 | tf_op jit(solution)/shard_map/ppermute | solution.py:20
  (104 shorter events, 19.7 us)
Async XLA Ops:
  0.0 0.7 copy-start
  0.0 0.7 copy-start.5
  0.9 12.7 %collective-permute-start = (f32[1,64,128]{2,1,0:T(8,128)S(1)}, f32[1,64,128]{2,1,0:T(8,128)S(1)}, u32[]{:S(2)}, u32[]{:S(2)}) collective-permute-start(f32[1,64,128]{2,1,0:T(8,128)S(1)} %get-tuple-element.47), channel_id=1, source_target_pairs={{0,8},{8,16},{16,24},{1,9},{9,17},{17,25},{2,10},{10,18},{18,26},{... | collective-permute-start | bytes 98312 | tf_op jit(solution)/shard_map/ppermute | solution.py:18
  4.4 9.1 %collective-permute-start.2 = (f32[1,1,64,128]{3,2,1,0:T(8,128)S(1)}, f32[1,1,64,128]{3,2,1,0:T(8,128)S(1)}, u32[]{:S(2)}, u32[]{:S(2)}) collective-permute-start(f32[1,1,64,128]{3,2,1,0:T(8,128)S(1)} %get-tuple-element.48), channel_id=1, source_target_pairs={{0,1},{1,2},{2,3},{3,4},{4,5},{5,6},{6,7},{8,9},{9,10},{10,11},{11... | collective-permute-start | bytes 98312 | tf_op jit(solution)/shard_map/ppermute | solution.py:18
  6.4 7.2 %collective-permute-start.3 = (f32[1,1,64,128]{3,2,1,0:T(8,128)S(1)}, f32[1,1,64,128]{3,2,1,0:T(8,128)S(1)}, u32[]{:S(2)}, u32[]{:S(2)}) collective-permute-start(f32[1,1,64,128]{3,2,1,0:T(8,128)S(1)} %get-tuple-element.49), channel_id=1, source_target_pairs={{1,0},{2,1},{3,2},{4,3},{5,4},{6,5},{7,6},{9,8},{10,9},{11,10},{12... | collective-permute-start | bytes 98312 | tf_op jit(solution)/shard_map/ppermute | solution.py:20
  10.9 5.8 %collective-permute-start.1 = (f32[1,64,128]{2,1,0:T(8,128)S(1)}, f32[1,64,128]{2,1,0:T(8,128)S(1)}, u32[]{:S(2)}, u32[]{:S(2)}) collective-permute-start(f32[1,64,128]{2,1,0:T(8,128)S(1)} %get-tuple-element.50), channel_id=1, source_target_pairs={{8,0},{16,8},{24,16},{9,1},{17,9},{25,17},{10,2},{18,10},{26,18},{... | collective-permute-start | bytes 98312 | tf_op jit(solution)/shard_map/ppermute | solution.py:20
  16.7 0.7 copy-start.2
  17.6 0.7 copy-start.4
  18.6 0.7 copy-start.6
  19.5 40.5 %copy-start.3 = (f32[6,48]{1,0:T(8,128)S(1)}, f32[6,48]{1,0:T(8,128)}, u32[]{:S(2)}) copy-start(f32[6,48]{1,0:T(8,128)} %param.15) | copy-start | bytes 3460
  69.7 7.1 %copy-start.1 = (bf16[1,1,512,512]{3,2,1,0:T(8,128)(2,1)S(1)}, bf16[1,1,512,512]{3,2,1,0:T(8,128)(2,1)}, u32[]{:S(2)}) copy-start(bf16[1,1,512,512]{3,2,1,0:T(8,128)(2,1)} %param.11) | copy-start | bytes 1572868
  70.4 10.2 %collective-permute-start.6 = (f32[1,1,64,128]{3,2,1,0:T(8,128)S(1)}, f32[1,1,64,128]{3,2,1,0:T(8,128)S(1)}, u32[]{:S(2)}, u32[]{:S(2)}) collective-permute-start(f32[1,1,64,128]{3,2,1,0:T(8,128)S(1)} %get-tuple-element.40), channel_id=1, source_target_pairs={{0,1},{1,2},{2,3},{3,4},{4,5},{5,6},{6,7},{8,9},{9,10},{10,11},{11... | collective-permute-start | bytes 98312 | tf_op jit(solution)/shard_map/ppermute | solution.py:18
  72.6 7.9 %collective-permute-start.7 = (f32[1,1,64,128]{3,2,1,0:T(8,128)S(1)}, f32[1,1,64,128]{3,2,1,0:T(8,128)S(1)}, u32[]{:S(2)}, u32[]{:S(2)}) collective-permute-start(f32[1,1,64,128]{3,2,1,0:T(8,128)S(1)} %get-tuple-element.41), channel_id=1, source_target_pairs={{1,0},{2,1},{3,2},{4,3},{5,4},{6,5},{7,6},{9,8},{10,9},{11,10},{12... | collective-permute-start | bytes 98312 | tf_op jit(solution)/shard_map/ppermute | solution.py:20
  77.1 3.7 %collective-permute-start.4 = (f32[1,64,128]{2,1,0:T(8,128)S(1)}, f32[1,64,128]{2,1,0:T(8,128)S(1)}, u32[]{:S(2)}, u32[]{:S(2)}) collective-permute-start(f32[1,64,128]{2,1,0:T(8,128)S(1)} %get-tuple-element.39), channel_id=1, source_target_pairs={{0,8},{8,16},{16,24},{1,9},{9,17},{17,25},{2,10},{10,18},{18,26},{... | collective-permute-start | bytes 98312 | tf_op jit(solution)/shard_map/ppermute | solution.py:18
  79.2 5.8 %collective-permute-start.5 = (f32[1,64,128]{2,1,0:T(8,128)S(1)}, f32[1,64,128]{2,1,0:T(8,128)S(1)}, u32[]{:S(2)}, u32[]{:S(2)}) collective-permute-start(f32[1,64,128]{2,1,0:T(8,128)S(1)} %get-tuple-element.42), channel_id=1, source_target_pairs={{8,0},{16,8},{24,16},{9,1},{17,9},{25,17},{10,2},{18,10},{26,18},{... | collective-permute-start | bytes 98312 | tf_op jit(solution)/shard_map/ppermute | solution.py:20
  86.0 10.8 %collective-permute-start.10 = (f32[1,1,64,128]{3,2,1,0:T(8,128)S(1)}, f32[1,1,64,128]{3,2,1,0:T(8,128)S(1)}, u32[]{:S(2)}, u32[]{:S(2)}) collective-permute-start(f32[1,1,64,128]{3,2,1,0:T(8,128)S(1)} %get-tuple-element.32), channel_id=1, source_target_pairs={{0,1},{1,2},{2,3},{3,4},{4,5},{5,6},{6,7},{8,9},{9,10},{10,11},{11... | collective-permute-start | bytes 98312 | tf_op jit(solution)/shard_map/ppermute | solution.py:18
  87.9 8.9 %collective-permute-start.11 = (f32[1,1,64,128]{3,2,1,0:T(8,128)S(1)}, f32[1,1,64,128]{3,2,1,0:T(8,128)S(1)}, u32[]{:S(2)}, u32[]{:S(2)}) collective-permute-start(f32[1,1,64,128]{3,2,1,0:T(8,128)S(1)} %get-tuple-element.33), channel_id=1, source_target_pairs={{1,0},{2,1},{3,2},{4,3},{5,4},{6,5},{7,6},{9,8},{10,9},{11,10},{12... | collective-permute-start | bytes 98312 | tf_op jit(solution)/shard_map/ppermute | solution.py:20
  92.5 4.6 %collective-permute-start.8 = (f32[1,64,128]{2,1,0:T(8,128)S(1)}, f32[1,64,128]{2,1,0:T(8,128)S(1)}, u32[]{:S(2)}, u32[]{:S(2)}) collective-permute-start(f32[1,64,128]{2,1,0:T(8,128)S(1)} %get-tuple-element.31), channel_id=1, source_target_pairs={{0,8},{8,16},{16,24},{1,9},{9,17},{17,25},{2,10},{10,18},{18,26},{... | collective-permute-start | bytes 98312 | tf_op jit(solution)/shard_map/ppermute | solution.py:18
  95.5 5.8 %collective-permute-start.9 = (f32[1,64,128]{2,1,0:T(8,128)S(1)}, f32[1,64,128]{2,1,0:T(8,128)S(1)}, u32[]{:S(2)}, u32[]{:S(2)}) collective-permute-start(f32[1,64,128]{2,1,0:T(8,128)S(1)} %get-tuple-element.34), channel_id=1, source_target_pairs={{8,0},{16,8},{24,16},{9,1},{17,9},{25,17},{10,2},{18,10},{26,18},{... | collective-permute-start | bytes 98312 | tf_op jit(solution)/shard_map/ppermute | solution.py:20
  153.3 9.7 %collective-permute-start.14 = (f32[1,1,64,128]{3,2,1,0:T(8,128)S(1)}, f32[1,1,64,128]{3,2,1,0:T(8,128)S(1)}, u32[]{:S(2)}, u32[]{:S(2)}) collective-permute-start(f32[1,1,64,128]{3,2,1,0:T(8,128)S(1)} %get-tuple-element.24), channel_id=1, source_target_pairs={{0,1},{1,2},{2,3},{3,4},{4,5},{5,6},{6,7},{8,9},{9,10},{10,11},{11... | collective-permute-start | bytes 98312 | tf_op jit(solution)/shard_map/ppermute | solution.py:18
  155.5 7.5 %collective-permute-start.15 = (f32[1,1,64,128]{3,2,1,0:T(8,128)S(1)}, f32[1,1,64,128]{3,2,1,0:T(8,128)S(1)}, u32[]{:S(2)}, u32[]{:S(2)}) collective-permute-start(f32[1,1,64,128]{3,2,1,0:T(8,128)S(1)} %get-tuple-element.25), channel_id=1, source_target_pairs={{1,0},{2,1},{3,2},{4,3},{5,4},{6,5},{7,6},{9,8},{10,9},{11,10},{12... | collective-permute-start | bytes 98312 | tf_op jit(solution)/shard_map/ppermute | solution.py:20
  159.8 3.5 %collective-permute-start.12 = (f32[1,64,128]{2,1,0:T(8,128)S(1)}, f32[1,64,128]{2,1,0:T(8,128)S(1)}, u32[]{:S(2)}, u32[]{:S(2)}) collective-permute-start(f32[1,64,128]{2,1,0:T(8,128)S(1)} %get-tuple-element.23), channel_id=1, source_target_pairs={{0,8},{8,16},{16,24},{1,9},{9,17},{17,25},{2,10},{10,18},{18,26},{... | collective-permute-start | bytes 98312 | tf_op jit(solution)/shard_map/ppermute | solution.py:18
  161.7 5.8 %collective-permute-start.13 = (f32[1,64,128]{2,1,0:T(8,128)S(1)}, f32[1,64,128]{2,1,0:T(8,128)S(1)}, u32[]{:S(2)}, u32[]{:S(2)}) collective-permute-start(f32[1,64,128]{2,1,0:T(8,128)S(1)} %get-tuple-element.26), channel_id=1, source_target_pairs={{8,0},{16,8},{24,16},{9,1},{17,9},{25,17},{10,2},{18,10},{26,18},{... | collective-permute-start | bytes 98312 | tf_op jit(solution)/shard_map/ppermute | solution.py:20
  168.5 10.3 %collective-permute-start.18 = (f32[1,1,64,128]{3,2,1,0:T(8,128)S(1)}, f32[1,1,64,128]{3,2,1,0:T(8,128)S(1)}, u32[]{:S(2)}, u32[]{:S(2)}) collective-permute-start(f32[1,1,64,128]{3,2,1,0:T(8,128)S(1)} %get-tuple-element.16), channel_id=1, source_target_pairs={{0,1},{1,2},{2,3},{3,4},{4,5},{5,6},{6,7},{8,9},{9,10},{10,11},{11... | collective-permute-start | bytes 98312 | tf_op jit(solution)/shard_map/ppermute | solution.py:18
  170.4 8.4 %collective-permute-start.19 = (f32[1,1,64,128]{3,2,1,0:T(8,128)S(1)}, f32[1,1,64,128]{3,2,1,0:T(8,128)S(1)}, u32[]{:S(2)}, u32[]{:S(2)}) collective-permute-start(f32[1,1,64,128]{3,2,1,0:T(8,128)S(1)} %get-tuple-element.17), channel_id=1, source_target_pairs={{1,0},{2,1},{3,2},{4,3},{5,4},{6,5},{7,6},{9,8},{10,9},{11,10},{12... | collective-permute-start | bytes 98312 | tf_op jit(solution)/shard_map/ppermute | solution.py:20
  175.0 4.1 %collective-permute-start.16 = (f32[1,64,128]{2,1,0:T(8,128)S(1)}, f32[1,64,128]{2,1,0:T(8,128)S(1)}, u32[]{:S(2)}, u32[]{:S(2)}) collective-permute-start(f32[1,64,128]{2,1,0:T(8,128)S(1)} %get-tuple-element.15), channel_id=1, source_target_pairs={{0,8},{8,16},{16,24},{1,9},{9,17},{17,25},{2,10},{10,18},{18,26},{... | collective-permute-start | bytes 98312 | tf_op jit(solution)/shard_map/ppermute | solution.py:18
  177.5 5.8 %collective-permute-start.17 = (f32[1,64,128]{2,1,0:T(8,128)S(1)}, f32[1,64,128]{2,1,0:T(8,128)S(1)}, u32[]{:S(2)}, u32[]{:S(2)}) collective-permute-start(f32[1,64,128]{2,1,0:T(8,128)S(1)} %get-tuple-element.18), channel_id=1, source_target_pairs={{8,0},{16,8},{24,16},{9,1},{17,9},{25,17},{10,2},{18,10},{26,18},{... | collective-permute-start | bytes 98312 | tf_op jit(solution)/shard_map/ppermute | solution.py:20
  235.3 9.7 %collective-permute-start.22 = (f32[1,1,64,128]{3,2,1,0:T(8,128)S(1)}, f32[1,1,64,128]{3,2,1,0:T(8,128)S(1)}, u32[]{:S(2)}, u32[]{:S(2)}) collective-permute-start(f32[1,1,64,128]{3,2,1,0:T(8,128)S(1)} %get-tuple-element.8), channel_id=1, source_target_pairs={{0,1},{1,2},{2,3},{3,4},{4,5},{5,6},{6,7},{8,9},{9,10},{10,11},{11... | collective-permute-start | bytes 98312 | tf_op jit(solution)/shard_map/ppermute | solution.py:18
  237.5 7.5 %collective-permute-start.23 = (f32[1,1,64,128]{3,2,1,0:T(8,128)S(1)}, f32[1,1,64,128]{3,2,1,0:T(8,128)S(1)}, u32[]{:S(2)}, u32[]{:S(2)}) collective-permute-start(f32[1,1,64,128]{3,2,1,0:T(8,128)S(1)} %get-tuple-element.9), channel_id=1, source_target_pairs={{1,0},{2,1},{3,2},{4,3},{5,4},{6,5},{7,6},{9,8},{10,9},{11,10},{12... | collective-permute-start | bytes 98312 | tf_op jit(solution)/shard_map/ppermute | solution.py:20
  241.7 3.5 %collective-permute-start.20 = (f32[1,64,128]{2,1,0:T(8,128)S(1)}, f32[1,64,128]{2,1,0:T(8,128)S(1)}, u32[]{:S(2)}, u32[]{:S(2)}) collective-permute-start(f32[1,64,128]{2,1,0:T(8,128)S(1)} %get-tuple-element.7), channel_id=1, source_target_pairs={{0,8},{8,16},{16,24},{1,9},{9,17},{17,25},{2,10},{10,18},{18,26},{... | collective-permute-start | bytes 98312 | tf_op jit(solution)/shard_map/ppermute | solution.py:18
  243.7 5.8 %collective-permute-start.21 = (f32[1,64,128]{2,1,0:T(8,128)S(1)}, f32[1,64,128]{2,1,0:T(8,128)S(1)}, u32[]{:S(2)}, u32[]{:S(2)}) collective-permute-start(f32[1,64,128]{2,1,0:T(8,128)S(1)} %get-tuple-element.10), channel_id=1, source_target_pairs={{8,0},{16,8},{24,16},{9,1},{17,9},{25,17},{10,2},{18,10},{26,18},{... | collective-permute-start | bytes 98312 | tf_op jit(solution)/shard_map/ppermute | solution.py:20
where the time goes:
time: 251 us; the launch traced here: 250 us
  blocking collectives  149 us (59%)
  starting transfers between devices  61.6 us (25%)
  waiting for transfers between devices  25.5 us (10%)
  matrix products  7.57 us (3%)
  local copies, waits for them, and re-layouts  4.4 us (2%)
    psum x3, blocking collectives, coarse_solve(): assembled = lax.psum(partial_value, ('sub', 'wide'))  121 us
    ppermute x12, starting transfers between devices, with_halo(): lax.ppermute(head, axis, [((i + 1) % count, i) for i in range(ends)])  34 us
    all_gather x3, blocking collectives, coarse_solve(): return lax.all_gather(owned_rows, 'wide', axis=1, tiled=True)  28 us
    ppermute x12, starting transfers between devices, with_halo(): lax.ppermute(tail, axis, [(i, (i + 1) % count) for i in range(ends)])  27.6 us
    ppermute x12, waiting for transfers between devices, with_halo(): lax.ppermute(head, axis, [((i + 1) % count, i) for i in range(ends)])  24.3 us
  transfers between devices with their start and end apart: 24, of which 11 were waited for; matrix products, arithmetic and copies ran while one was open for 1% of the time, Pallas kernels for 0%

commit v1 on v0

--- a/solution.py
+++ b/solution.py
@@ -53,7 +53,7 @@
 
 
 def coarse_solve(partial_value, coarse_inverse):
-    assembled = lax.psum(partial_value, ("sub", "wide"))
+    assembled = jnp.sum(lax.all_gather(partial_value, ("sub", "wide")), axis=0)
     owned_rows = jnp.dot(assembled, coarse_inverse.T, precision=lax.Precision.HIGHEST)
     return lax.all_gather(owned_rows, "wide", axis=1, tiled=True)
 

time: 251 us -> 240 us (0.956)
  blocking collectives: 149 us -> 142 us
  starting transfers between devices: 61.6 us -> 57.1 us
    psum x3 -> x0, blocking collectives: 121 us -> none  [coarse_solve(): assembled = lax.psum(partial_value, ('sub', 'wide'))]
    all_gather x0 -> x3, blocking collectives: none -> 107 us  [coarse_solve(): assembled = jnp.sum(lax.all_gather(partial_value, ('sub', 'wide')), axis=0)]
    all_gather x3, blocking collectives: 28 us -> 35.4 us  [coarse_solve(): return lax.all_gather(owned_rows, 'wide', axis=1, tiled=True)]
    ppermute x12, starting transfers between devices: 27.6 us -> 23.1 us  [with_halo(): lax.ppermute(tail, axis, [(i, (i + 1) % count) for i in range(ends)])]
where the time goes in v1:
time: 240 us; the launch traced here: 239 us
  blocking collectives  142 us (59%)
  starting transfers between devices  57.1 us (24%)
  waiting for transfers between devices  25.5 us (11%)
  matrix products  7.58 us (3%)
  local copies, waits for them, and re-layouts  5.01 us (2%)
    all_gather x3, blocking collectives, coarse_solve(): assembled = jnp.sum(lax.all_gather(partial_value, ('sub', 'wide')), axis=0)  107 us
    all_gather x3, blocking collectives, coarse_solve(): return lax.all_gather(owned_rows, 'wide', axis=1, tiled=True)  35.4 us
    ppermute x12, starting transfers between devices, with_halo(): lax.ppermute(head, axis, [((i + 1) % count, i) for i in range(ends)])  34 us
    ppermute x12, waiting for transfers between devices, with_halo(): lax.ppermute(head, axis, [((i + 1) % count, i) for i in range(ends)])  24.3 us
    ppermute x12, starting transfers between devices, with_halo(): lax.ppermute(tail, axis, [(i, (i + 1) % count) for i in range(ends)])  23.1 us
  transfers between devices with their start and end apart: 24, of which 11 were waited for; matrix products, arithmetic and copies ran while one was open for 1% of the time, Pallas kernels for 0%

profile of v1, /device:TPU:4, one launch (start us, length us, event | category | flops | bytes accessed | tf_op | source)
XLA Modules:
  0.0 239.4 jit_solution(16813809174395622771)
XLA Ops:
  0.9 3.5 %collective-permute-start = (f32[1,64,128]{2,1,0:T(8,128)S(1)}, f32[1,64,128]{2,1,0:T(8,128)S(1)}, u32[]{:S(2)}, u32[]{:S(2)}) collective-permute-start(f32[1,64,128]{2,1,0:T(8,128)S(1)} %get-tuple-element.47), channel_id=1, source_target_pairs={{0,8},{8,16},{16,24},{1,9},{9,17},{17,25},{2,10},{10,18},{18,26},{... | collective-permute-start | bytes 98312 | tf_op jit(solution)/shard_map/ppermute | solution.py:18
  4.4 1.9 collective-permute-start.2
  6.4 4.5 %collective-permute-start.3 = (f32[1,1,64,128]{3,2,1,0:T(8,128)S(1)}, f32[1,1,64,128]{3,2,1,0:T(8,128)S(1)}, u32[]{:S(2)}, u32[]{:S(2)}) collective-permute-start(f32[1,1,64,128]{3,2,1,0:T(8,128)S(1)} %get-tuple-element.49), channel_id=1, source_target_pairs={{1,0},{2,1},{3,2},{4,3},{5,4},{6,5},{7,6},{9,8},{10,9},{11,10},{12... | collective-permute-start | bytes 98312 | tf_op jit(solution)/shard_map/ppermute | solution.py:20
  10.9 1.3 collective-permute-start.1
  13.6 3.1 %collective-permute-done.1 = f32[1,64,128]{2,1,0:T(8,128)S(1)} collective-permute-done((f32[1,64,128]{2,1,0:T(8,128)S(1)}, f32[1,64,128]{2,1,0:T(8,128)S(1)}, u32[]{:S(2)}, u32[]{:S(2)}) %collective-permute-start.1) | collective-permute-done | bytes 32800 | tf_op jit(solution)/shard_map/ppermute | solution.py:20
  20.2 37.6 %all-gather.3 = f32[32,64,48]{1,2,0:T(8,128)S(1)} all-gather(f32[1,64,48]{1,2,0:T(8,128)S(1)} %convolution_bitcast_fusion.6), channel_id=2, replica_groups=mesh['sub'=4,'wide'=8] {'sub','wide'}, dimensions={0}, use_global_device_ids=true | all-gather | bytes 405504 | tf_op jit(solution)/shard_map/all_gather | solution.py:56
  58.6 11.9 %all-gather.4 = f32[8,6,64]{2,1,0:T(8,128)S(1)} all-gather(f32[1,6,64]{2,1,0:T(8,128)S(1)} %convolution_bitcast_fusion.9), channel_id=1, replica_groups=mesh['sub'=4,'wide'=8] {'wide'}, dimensions={0}, use_global_device_ids=true | all-gather | bytes 13824 | tf_op jit(solution)/shard_map/all_gather | solution.py:58
  71.0 2.3 collective-permute-start.6
  73.2 4.2 %collective-permute-start.7 = (f32[1,1,64,128]{3,2,1,0:T(8,128)S(1)}, f32[1,1,64,128]{3,2,1,0:T(8,128)S(1)}, u32[]{:S(2)}, u32[]{:S(2)}) collective-permute-start(f32[1,1,64,128]{3,2,1,0:T(8,128)S(1)} %get-tuple-element.41), channel_id=1, source_target_pairs={{1,0},{2,1},{3,2},{4,3},{5,4},{6,5},{7,6},{9,8},{10,9},{11,10},{12... | collective-permute-start | bytes 98312 | tf_op jit(solution)/shard_map/ppermute | solution.py:20
  79.0 1.3 collective-permute-start.5
  80.6 4.2 %collective-permute-done.5 = f32[1,64,128]{2,1,0:T(8,128)S(1)} collective-permute-done((f32[1,64,128]{2,1,0:T(8,128)S(1)}, f32[1,64,128]{2,1,0:T(8,128)S(1)}, u32[]{:S(2)}, u32[]{:S(2)}) %collective-permute-start.5) | collective-permute-done | bytes 32800 | tf_op jit(solution)/shard_map/ppermute | solution.py:20
  85.8 1.9 collective-permute-start.10
  87.7 4.5 %collective-permute-start.11 = (f32[1,1,64,128]{3,2,1,0:T(8,128)S(1)}, f32[1,1,64,128]{3,2,1,0:T(8,128)S(1)}, u32[]{:S(2)}, u32[]{:S(2)}) collective-permute-start(f32[1,1,64,128]{3,2,1,0:T(8,128)S(1)} %get-tuple-element.33), channel_id=1, source_target_pairs={{1,0},{2,1},{3,2},{4,3},{5,4},{6,5},{7,6},{9,8},{10,9},{11,10},{12... | collective-permute-start | bytes 98312 | tf_op jit(solution)/shard_map/ppermute | solution.py:20
  92.2 1.6 collective-permute-start.8
  93.9 1.3 collective-permute-start.9
  95.4 4.2 %collective-permute-done.9 = f32[1,64,128]{2,1,0:T(8,128)S(1)} collective-permute-done((f32[1,64,128]{2,1,0:T(8,128)S(1)}, f32[1,64,128]{2,1,0:T(8,128)S(1)}, u32[]{:S(2)}, u32[]{:S(2)}) %collective-permute-start.9) | collective-permute-done | bytes 32800 | tf_op jit(solution)/shard_map/ppermute | solution.py:20
  101.2 34.5 %all-gather.5 = f32[32,64,48]{1,2,0:T(8,128)S(1)} all-gather(f32[1,64,48]{1,2,0:T(8,128)S(1)} %convolution_bitcast_fusion.5), channel_id=3, replica_groups=mesh['sub'=4,'wide'=8] {'sub','wide'}, dimensions={0}, use_global_device_ids=true | all-gather | bytes 405504 | tf_op jit(solution)/shard_map/all_gather | solution.py:56
  135.9 11.8 %all-gather.6 = f32[8,6,64]{2,1,0:T(8,128)S(1)} all-gather(f32[1,6,64]{2,1,0:T(8,128)S(1)} %convolution_bitcast_fusion.8), channel_id=1, replica_groups=mesh['sub'=4,'wide'=8] {'wide'}, dimensions={0}, use_global_device_ids=true | all-gather | bytes 13824 | tf_op jit(solution)/shard_map/all_gather | solution.py:58
  148.2 2.3 collective-permute-start.14
  150.4 4.2 %collective-permute-start.15 = (f32[1,1,64,128]{3,2,1,0:T(8,128)S(1)}, f32[1,1,64,128]{3,2,1,0:T(8,128)S(1)}, u32[]{:S(2)}, u32[]{:S(2)}) collective-permute-start(f32[1,1,64,128]{3,2,1,0:T(8,128)S(1)} %get-tuple-element.25), channel_id=1, source_target_pairs={{1,0},{2,1},{3,2},{4,3},{5,4},{6,5},{7,6},{9,8},{10,9},{11,10},{12... | collective-permute-start | bytes 98312 | tf_op jit(solution)/shard_map/ppermute | solution.py:20
  155.9 1.3 collective-permute-start.13
  157.5 4.2 %collective-permute-done.13 = f32[1,64,128]{2,1,0:T(8,128)S(1)} collective-permute-done((f32[1,64,128]{2,1,0:T(8,128)S(1)}, f32[1,64,128]{2,1,0:T(8,128)S(1)}, u32[]{:S(2)}, u32[]{:S(2)}) %collective-permute-start.13) | collective-permute-done | bytes 32800 | tf_op jit(solution)/shard_map/ppermute | solution.py:20
  162.7 1.9 collective-permute-start.18
  164.6 4.5 %collective-permute-start.19 = (f32[1,1,64,128]{3,2,1,0:T(8,128)S(1)}, f32[1,1,64,128]{3,2,1,0:T(8,128)S(1)}, u32[]{:S(2)}, u32[]{:S(2)}) collective-permute-start(f32[1,1,64,128]{3,2,1,0:T(8,128)S(1)} %get-tuple-element.17), channel_id=1, source_target_pairs={{1,0},{2,1},{3,2},{4,3},{5,4},{6,5},{7,6},{9,8},{10,9},{11,10},{12... | collective-permute-start | bytes 98312 | tf_op jit(solution)/shard_map/ppermute | solution.py:20
  169.2 1.6 collective-permute-start.16
  170.8 1.3 collective-permute-start.17
  172.4 4.2 %collective-permute-done.17 = f32[1,64,128]{2,1,0:T(8,128)S(1)} collective-permute-done((f32[1,64,128]{2,1,0:T(8,128)S(1)}, f32[1,64,128]{2,1,0:T(8,128)S(1)}, u32[]{:S(2)}, u32[]{:S(2)}) %collective-permute-start.17) | collective-permute-done | bytes 32800 | tf_op jit(solution)/shard_map/ppermute | solution.py:20
  178.1 34.5 %all-gather.7 = f32[32,64,48]{1,2,0:T(8,128)S(1)} all-gather(f32[1,64,48]{1,2,0:T(8,128)S(1)} %convolution_bitcast_fusion.4), channel_id=4, replica_groups=mesh['sub'=4,'wide'=8] {'sub','wide'}, dimensions={0}, use_global_device_ids=true | all-gather | bytes 405504 | tf_op jit(solution)/shard_map/all_gather | solution.py:56
  212.9 11.8 %all-gather.8 = f32[8,6,64]{2,1,0:T(8,128)S(1)} all-gather(f32[1,6,64]{2,1,0:T(8,128)S(1)} %convolution_bitcast_fusion.7), channel_id=1, replica_groups=mesh['sub'=4,'wide'=8] {'wide'}, dimensions={0}, use_global_device_ids=true | all-gather | bytes 13824 | tf_op jit(solution)/shard_map/all_gather | solution.py:58
  225.1 2.3 collective-permute-start.22
  227.4 4.2 %collective-permute-start.23 = (f32[1,1,64,128]{3,2,1,0:T(8,128)S(1)}, f32[1,1,64,128]{3,2,1,0:T(8,128)S(1)}, u32[]{:S(2)}, u32[]{:S(2)}) collective-permute-start(f32[1,1,64,128]{3,2,1,0:T(8,128)S(1)} %get-tuple-element.9), channel_id=1, source_target_pairs={{1,0},{2,1},{3,2},{4,3},{5,4},{6,5},{7,6},{9,8},{10,9},{11,10},{12... | collective-permute-start | bytes 98312 | tf_op jit(solution)/shard_map/ppermute | solution.py:20
  234.5 4.2 %collective-permute-done.21 = f32[1,64,128]{2,1,0:T(8,128)S(1)} collective-permute-done((f32[1,64,128]{2,1,0:T(8,128)S(1)}, f32[1,64,128]{2,1,0:T(8,128)S(1)}, u32[]{:S(2)}, u32[]{:S(2)}) %collective-permute-start.21) | collective-permute-done | bytes 32800 | tf_op jit(solution)/shard_map/ppermute | solution.py:20
  (107 shorter events, 20.5 us)
Async XLA Ops:
  0.0 0.7 copy-start
  0.0 0.7 copy-start.5
  0.9 12.7 %collective-permute-start = (f32[1,64,128]{2,1,0:T(8,128)S(1)}, f32[1,64,128]{2,1,0:T(8,128)S(1)}, u32[]{:S(2)}, u32[]{:S(2)}) collective-permute-start(f32[1,64,128]{2,1,0:T(8,128)S(1)} %get-tuple-element.47), channel_id=1, source_target_pairs={{0,8},{8,16},{16,24},{1,9},{9,17},{17,25},{2,10},{10,18},{18,26},{... | collective-permute-start | bytes 98312 | tf_op jit(solution)/shard_map/ppermute | solution.py:18
  4.4 9.1 %collective-permute-start.2 = (f32[1,1,64,128]{3,2,1,0:T(8,128)S(1)}, f32[1,1,64,128]{3,2,1,0:T(8,128)S(1)}, u32[]{:S(2)}, u32[]{:S(2)}) collective-permute-start(f32[1,1,64,128]{3,2,1,0:T(8,128)S(1)} %get-tuple-element.48), channel_id=1, source_target_pairs={{0,1},{1,2},{2,3},{3,4},{4,5},{5,6},{6,7},{8,9},{9,10},{10,11},{11... | collective-permute-start | bytes 98312 | tf_op jit(solution)/shard_map/ppermute | solution.py:18
  6.4 7.2 %collective-permute-start.3 = (f32[1,1,64,128]{3,2,1,0:T(8,128)S(1)}, f32[1,1,64,128]{3,2,1,0:T(8,128)S(1)}, u32[]{:S(2)}, u32[]{:S(2)}) collective-permute-start(f32[1,1,64,128]{3,2,1,0:T(8,128)S(1)} %get-tuple-element.49), channel_id=1, source_target_pairs={{1,0},{2,1},{3,2},{4,3},{5,4},{6,5},{7,6},{9,8},{10,9},{11,10},{12... | collective-permute-start | bytes 98312 | tf_op jit(solution)/shard_map/ppermute | solution.py:20
  10.9 5.8 %collective-permute-start.1 = (f32[1,64,128]{2,1,0:T(8,128)S(1)}, f32[1,64,128]{2,1,0:T(8,128)S(1)}, u32[]{:S(2)}, u32[]{:S(2)}) collective-permute-start(f32[1,64,128]{2,1,0:T(8,128)S(1)} %get-tuple-element.50), channel_id=1, source_target_pairs={{8,0},{16,8},{24,16},{9,1},{17,9},{25,17},{10,2},{18,10},{26,18},{... | collective-permute-start | bytes 98312 | tf_op jit(solution)/shard_map/ppermute | solution.py:20
  16.7 0.7 copy-start.2
  17.6 0.7 copy-start.4
  19.2 0.7 copy-start.6
  57.8 0.7 copy-start.3
  58.5 19.0 %copy-start.1 = (bf16[1,1,512,512]{3,2,1,0:T(8,128)(2,1)S(1)}, bf16[1,1,512,512]{3,2,1,0:T(8,128)(2,1)}, u32[]{:S(2)}) copy-start(bf16[1,1,512,512]{3,2,1,0:T(8,128)(2,1)} %param.11) | copy-start | bytes 1572868
  71.0 9.3 %collective-permute-start.6 = (f32[1,1,64,128]{3,2,1,0:T(8,128)S(1)}, f32[1,1,64,128]{3,2,1,0:T(8,128)S(1)}, u32[]{:S(2)}, u32[]{:S(2)}) collective-permute-start(f32[1,1,64,128]{3,2,1,0:T(8,128)S(1)} %get-tuple-element.40), channel_id=1, source_target_pairs={{0,1},{1,2},{2,3},{3,4},{4,5},{5,6},{6,7},{8,9},{9,10},{10,11},{11... | collective-permute-start | bytes 98312 | tf_op jit(solution)/shard_map/ppermute | solution.py:18
  73.2 7.1 %collective-permute-start.7 = (f32[1,1,64,128]{3,2,1,0:T(8,128)S(1)}, f32[1,1,64,128]{3,2,1,0:T(8,128)S(1)}, u32[]{:S(2)}, u32[]{:S(2)}) collective-permute-start(f32[1,1,64,128]{3,2,1,0:T(8,128)S(1)} %get-tuple-element.41), channel_id=1, source_target_pairs={{1,0},{2,1},{3,2},{4,3},{5,4},{6,5},{7,6},{9,8},{10,9},{11,10},{12... | collective-permute-start | bytes 98312 | tf_op jit(solution)/shard_map/ppermute | solution.py:20
  77.7 2.9 %collective-permute-start.4 = (f32[1,64,128]{2,1,0:T(8,128)S(1)}, f32[1,64,128]{2,1,0:T(8,128)S(1)}, u32[]{:S(2)}, u32[]{:S(2)}) collective-permute-start(f32[1,64,128]{2,1,0:T(8,128)S(1)} %get-tuple-element.39), channel_id=1, source_target_pairs={{0,8},{8,16},{16,24},{1,9},{9,17},{17,25},{2,10},{10,18},{18,26},{... | collective-permute-start | bytes 98312 | tf_op jit(solution)/shard_map/ppermute | solution.py:18
  79.0 5.8 %collective-permute-start.5 = (f32[1,64,128]{2,1,0:T(8,128)S(1)}, f32[1,64,128]{2,1,0:T(8,128)S(1)}, u32[]{:S(2)}, u32[]{:S(2)}) collective-permute-start(f32[1,64,128]{2,1,0:T(8,128)S(1)} %get-tuple-element.42), channel_id=1, source_target_pairs={{8,0},{16,8},{24,16},{9,1},{17,9},{25,17},{10,2},{18,10},{26,18},{... | collective-permute-start | bytes 98312 | tf_op jit(solution)/shard_map/ppermute | solution.py:20
  85.8 9.4 %collective-permute-start.10 = (f32[1,1,64,128]{3,2,1,0:T(8,128)S(1)}, f32[1,1,64,128]{3,2,1,0:T(8,128)S(1)}, u32[]{:S(2)}, u32[]{:S(2)}) collective-permute-start(f32[1,1,64,128]{3,2,1,0:T(8,128)S(1)} %get-tuple-element.32), channel_id=1, source_target_pairs={{0,1},{1,2},{2,3},{3,4},{4,5},{5,6},{6,7},{8,9},{9,10},{10,11},{11... | collective-permute-start | bytes 98312 | tf_op jit(solution)/shard_map/ppermute | solution.py:18
  87.7 7.5 %collective-permute-start.11 = (f32[1,1,64,128]{3,2,1,0:T(8,128)S(1)}, f32[1,1,64,128]{3,2,1,0:T(8,128)S(1)}, u32[]{:S(2)}, u32[]{:S(2)}) collective-permute-start(f32[1,1,64,128]{3,2,1,0:T(8,128)S(1)} %get-tuple-element.33), channel_id=1, source_target_pairs={{1,0},{2,1},{3,2},{4,3},{5,4},{6,5},{7,6},{9,8},{10,9},{11,10},{12... | collective-permute-start | bytes 98312 | tf_op jit(solution)/shard_map/ppermute | solution.py:20
  92.2 3.2 %collective-permute-start.8 = (f32[1,64,128]{2,1,0:T(8,128)S(1)}, f32[1,64,128]{2,1,0:T(8,128)S(1)}, u32[]{:S(2)}, u32[]{:S(2)}) collective-permute-start(f32[1,64,128]{2,1,0:T(8,128)S(1)} %get-tuple-element.31), channel_id=1, source_target_pairs={{0,8},{8,16},{16,24},{1,9},{9,17},{17,25},{2,10},{10,18},{18,26},{... | collective-permute-start | bytes 98312 | tf_op jit(solution)/shard_map/ppermute | solution.py:18
  93.9 5.8 %collective-permute-start.9 = (f32[1,64,128]{2,1,0:T(8,128)S(1)}, f32[1,64,128]{2,1,0:T(8,128)S(1)}, u32[]{:S(2)}, u32[]{:S(2)}) collective-permute-start(f32[1,64,128]{2,1,0:T(8,128)S(1)} %get-tuple-element.34), channel_id=1, source_target_pairs={{8,0},{16,8},{24,16},{9,1},{17,9},{25,17},{10,2},{18,10},{26,18},{... | collective-permute-start | bytes 98312 | tf_op jit(solution)/shard_map/ppermute | solution.py:20
  148.2 9.1 %collective-permute-start.14 = (f32[1,1,64,128]{3,2,1,0:T(8,128)S(1)}, f32[1,1,64,128]{3,2,1,0:T(8,128)S(1)}, u32[]{:S(2)}, u32[]{:S(2)}) collective-permute-start(f32[1,1,64,128]{3,2,1,0:T(8,128)S(1)} %get-tuple-element.24), channel_id=1, source_target_pairs={{0,1},{1,2},{2,3},{3,4},{4,5},{5,6},{6,7},{8,9},{9,10},{10,11},{11... | collective-permute-start | bytes 98312 | tf_op jit(solution)/shard_map/ppermute | solution.py:18
  150.4 6.8 %collective-permute-start.15 = (f32[1,1,64,128]{3,2,1,0:T(8,128)S(1)}, f32[1,1,64,128]{3,2,1,0:T(8,128)S(1)}, u32[]{:S(2)}, u32[]{:S(2)}) collective-permute-start(f32[1,1,64,128]{3,2,1,0:T(8,128)S(1)} %get-tuple-element.25), channel_id=1, source_target_pairs={{1,0},{2,1},{3,2},{4,3},{5,4},{6,5},{7,6},{9,8},{10,9},{11,10},{12... | collective-permute-start | bytes 98312 | tf_op jit(solution)/shard_map/ppermute | solution.py:20
  154.6 2.9 %collective-permute-start.12 = (f32[1,64,128]{2,1,0:T(8,128)S(1)}, f32[1,64,128]{2,1,0:T(8,128)S(1)}, u32[]{:S(2)}, u32[]{:S(2)}) collective-permute-start(f32[1,64,128]{2,1,0:T(8,128)S(1)} %get-tuple-element.23), channel_id=1, source_target_pairs={{0,8},{8,16},{16,24},{1,9},{9,17},{17,25},{2,10},{10,18},{18,26},{... | collective-permute-start | bytes 98312 | tf_op jit(solution)/shard_map/ppermute | solution.py:18
  155.9 5.8 %collective-permute-start.13 = (f32[1,64,128]{2,1,0:T(8,128)S(1)}, f32[1,64,128]{2,1,0:T(8,128)S(1)}, u32[]{:S(2)}, u32[]{:S(2)}) collective-permute-start(f32[1,64,128]{2,1,0:T(8,128)S(1)} %get-tuple-element.26), channel_id=1, source_target_pairs={{8,0},{16,8},{24,16},{9,1},{17,9},{25,17},{10,2},{18,10},{26,18},{... | collective-permute-start | bytes 98312 | tf_op jit(solution)/shard_map/ppermute | solution.py:20
  162.7 9.4 %collective-permute-start.18 = (f32[1,1,64,128]{3,2,1,0:T(8,128)S(1)}, f32[1,1,64,128]{3,2,1,0:T(8,128)S(1)}, u32[]{:S(2)}, u32[]{:S(2)}) collective-permute-start(f32[1,1,64,128]{3,2,1,0:T(8,128)S(1)} %get-tuple-element.16), channel_id=1, source_target_pairs={{0,1},{1,2},{2,3},{3,4},{4,5},{5,6},{6,7},{8,9},{9,10},{10,11},{11... | collective-permute-start | bytes 98312 | tf_op jit(solution)/shard_map/ppermute | solution.py:18
  164.6 7.5 %collective-permute-start.19 = (f32[1,1,64,128]{3,2,1,0:T(8,128)S(1)}, f32[1,1,64,128]{3,2,1,0:T(8,128)S(1)}, u32[]{:S(2)}, u32[]{:S(2)}) collective-permute-start(f32[1,1,64,128]{3,2,1,0:T(8,128)S(1)} %get-tuple-element.17), channel_id=1, source_target_pairs={{1,0},{2,1},{3,2},{4,3},{5,4},{6,5},{7,6},{9,8},{10,9},{11,10},{12... | collective-permute-start | bytes 98312 | tf_op jit(solution)/shard_map/ppermute | solution.py:20
  169.2 3.2 %collective-permute-start.16 = (f32[1,64,128]{2,1,0:T(8,128)S(1)}, f32[1,64,128]{2,1,0:T(8,128)S(1)}, u32[]{:S(2)}, u32[]{:S(2)}) collective-permute-start(f32[1,64,128]{2,1,0:T(8,128)S(1)} %get-tuple-element.15), channel_id=1, source_target_pairs={{0,8},{8,16},{16,24},{1,9},{9,17},{17,25},{2,10},{10,18},{18,26},{... | collective-permute-start | bytes 98312 | tf_op jit(solution)/shard_map/ppermute | solution.py:18
  170.8 5.8 %collective-permute-start.17 = (f32[1,64,128]{2,1,0:T(8,128)S(1)}, f32[1,64,128]{2,1,0:T(8,128)S(1)}, u32[]{:S(2)}, u32[]{:S(2)}) collective-permute-start(f32[1,64,128]{2,1,0:T(8,128)S(1)} %get-tuple-element.18), channel_id=1, source_target_pairs={{8,0},{16,8},{24,16},{9,1},{17,9},{25,17},{10,2},{18,10},{26,18},{... | collective-permute-start | bytes 98312 | tf_op jit(solution)/shard_map/ppermute | solution.py:20
  225.1 9.1 %collective-permute-start.22 = (f32[1,1,64,128]{3,2,1,0:T(8,128)S(1)}, f32[1,1,64,128]{3,2,1,0:T(8,128)S(1)}, u32[]{:S(2)}, u32[]{:S(2)}) collective-permute-start(f32[1,1,64,128]{3,2,1,0:T(8,128)S(1)} %get-tuple-element.8), channel_id=1, source_target_pairs={{0,1},{1,2},{2,3},{3,4},{4,5},{5,6},{6,7},{8,9},{9,10},{10,11},{11... | collective-permute-start | bytes 98312 | tf_op jit(solution)/shard_map/ppermute | solution.py:18
  227.4 6.8 %collective-permute-start.23 = (f32[1,1,64,128]{3,2,1,0:T(8,128)S(1)}, f32[1,1,64,128]{3,2,1,0:T(8,128)S(1)}, u32[]{:S(2)}, u32[]{:S(2)}) collective-permute-start(f32[1,1,64,128]{3,2,1,0:T(8,128)S(1)} %get-tuple-element.9), channel_id=1, source_target_pairs={{1,0},{2,1},{3,2},{4,3},{5,4},{6,5},{7,6},{9,8},{10,9},{11,10},{12... | collective-permute-start | bytes 98312 | tf_op jit(solution)/shard_map/ppermute | solution.py:20
  231.6 2.9 %collective-permute-start.20 = (f32[1,64,128]{2,1,0:T(8,128)S(1)}, f32[1,64,128]{2,1,0:T(8,128)S(1)}, u32[]{:S(2)}, u32[]{:S(2)}) collective-permute-start(f32[1,64,128]{2,1,0:T(8,128)S(1)} %get-tuple-element.7), channel_id=1, source_target_pairs={{0,8},{8,16},{16,24},{1,9},{9,17},{17,25},{2,10},{10,18},{18,26},{... | collective-permute-start | bytes 98312 | tf_op jit(solution)/shard_map/ppermute | solution.py:18
  232.9 5.8 %collective-permute-start.21 = (f32[1,64,128]{2,1,0:T(8,128)S(1)}, f32[1,64,128]{2,1,0:T(8,128)S(1)}, u32[]{:S(2)}, u32[]{:S(2)}) collective-permute-start(f32[1,64,128]{2,1,0:T(8,128)S(1)} %get-tuple-element.10), channel_id=1, source_target_pairs={{8,0},{16,8},{24,16},{9,1},{17,9},{25,17},{10,2},{18,10},{26,18},{... | collective-permute-start | bytes 98312 | tf_op jit(solution)/shard_map/ppermute | solution.py:20
